TPU v7x, 32 devices: a whole 2x2x4 slice. The times are simulated.
32 devices in a mesh: orb: 8 (over z, x), grid: 4 (over y, core).
Axes of the slice: x: 2, y: 2, z: 4, core: 2. Of those that a mesh axis runs over, the one named last changes fastest.
Arguments:
- potentials: float32 [8, 2, 4, 64, 1024], P('orb', None, None, 'grid'), may hold values from -6 to 6
- orbitals: float32 [32, 64, 1024], P('orb', 'grid'), may hold values from -6 to 6
- local_pot: float32 [64, 1024], P('grid'), may hold values from 0 to 1
- shifts: float32 [32], P('orb'), may hold values from 0.75 to 2
- occupation: int32 [32], P('orb'), may hold values from 1 to 2
- owner: int32 [2], replicated, may hold values from 0 to 7
Outputs:
- response: float32 [8, 2, 4, 64, 1024], P('orb', None, None, 'grid')
All inputs are finite; a program needn't handle non-finite values.
Results may differ from a plain program's by a relative error of at most 0.00002.
Values sent between devices are 32-bit elements; how exact they have to be, the bound alone decides.
A program may use at most 64 MiB of HBM per device.

v0:
```python
import jax
import jax.numpy as jnp
from jax import lax
from jax.sharding import PartitionSpec as P

NZ = 32
ITERS = 4
NEAR_COEF = 4.0 / 3.0
FAR_COEF = -1.0 / 12.0
CENTER_COEF = -2.5
KINETIC_DIAG = 3.75


def with_halo(cells, sides, width):
    for axis, dim in sides:
        count = lax.axis_size(axis)
        ends = count - 1
        head = lax.slice_in_dim(cells, 0, width, axis=dim)
        tail = lax.slice_in_dim(cells, cells.shape[dim] - width, cells.shape[dim], axis=dim)
        cells = jnp.concatenate(
            [
                lax.ppermute(tail, axis, [(i, (i + 1) % count) for i in range(ends)]),
                cells,
                lax.ppermute(head, axis, [((i + 1) % count, i) for i in range(ends)]),
            ],
            axis=dim,
        )
    return cells


def from_root(value, axis, source):
    kept = jnp.where(lax.axis_index(axis) == source, value, 0).astype(value.dtype)
    return lax.psum(kept, axis)


def laplacian(padded, solution):
    cell_rows = solution.shape[-2]
    plane_cells = solution.shape[-1]
    along_rows = NEAR_COEF * (
        padded[..., 1 : cell_rows + 1, :] + padded[..., 3 : cell_rows + 3, :]
    ) + FAR_COEF * (padded[..., 0:cell_rows, :] + padded[..., 4 : cell_rows + 4, :])
    widths = [(0, 0)] * (solution.ndim - 1)
    padded_cols = jnp.pad(solution, widths + [(2 * NZ, 2 * NZ)])
    along_cols = NEAR_COEF * (
        padded_cols[..., NZ : NZ + plane_cells] + padded_cols[..., 3 * NZ : 3 * NZ + plane_cells]
    ) + FAR_COEF * (
        padded_cols[..., 0:plane_cells] + padded_cols[..., 4 * NZ : 4 * NZ + plane_cells]
    )
    padded_depth = jnp.pad(solution, widths + [(2, 2)])
    z_index = jnp.arange(plane_cells, dtype=jnp.int32) % NZ
    lower_one = (z_index >= 1).astype(solution.dtype)
    upper_one = (z_index <= NZ - 2).astype(solution.dtype)
    lower_two = (z_index >= 2).astype(solution.dtype)
    upper_two = (z_index <= NZ - 3).astype(solution.dtype)
    along_depth = NEAR_COEF * (
        padded_depth[..., 1 : plane_cells + 1] * lower_one
        + padded_depth[..., 3 : plane_cells + 3] * upper_one
    ) + FAR_COEF * (
        padded_depth[..., 0:plane_cells] * lower_two
        + padded_depth[..., 4 : plane_cells + 4] * upper_two
    )
    return along_rows + along_cols + along_depth + 3.0 * CENTER_COEF * solution


def sweep(padded, solution, source, potential, diagonal):
    applied = -0.5 * laplacian(padded, solution) + potential * solution
    return solution + (source - applied) / diagonal


def shards(potentials, orbitals, local_pot, shifts, occupation, owner):
    cell_rows = orbitals.shape[1]
    orbital_count = orbitals.shape[0]
    position = lax.axis_index("orb")
    weights = occupation.astype(jnp.float32)
    stored = potentials[0]
    block_count = stored.shape[0]
    results = []
    for block_index in range(block_count):
        trials = from_root(stored[block_index], "orb", owner[block_index])
        halo_depth = 2 * ITERS
        trial_count = trials.shape[0]
        stacked = jnp.concatenate([orbitals, trials, local_pot[None]], axis=0)
        extended = with_halo(stacked, (("grid", 1),), halo_depth)
        orbit_ext = extended[:orbital_count]
        trial_ext = extended[orbital_count : orbital_count + trial_count]
        local_ext = extended[orbital_count + trial_count]
        source_ext = -(trial_ext[None] * orbit_ext[:, None])
        potential_ext = local_ext[None, None] + shifts[:, None, None, None]
        diagonal_ext = KINETIC_DIAG + potential_ext
        global_rows = (
            lax.axis_index("grid") * cell_rows
            - halo_depth
            + jnp.arange(cell_rows + 2 * halo_depth, dtype=jnp.int32)
        )
        inside = ((global_rows >= 0) & (global_rows < cell_rows * lax.axis_size("grid"))).astype(
            jnp.float32
        )[:, None]
        solution_ext = source_ext / diagonal_ext
        for repeat in range(ITERS):
            margin = 2 * (repeat + 1)
            extent = cell_rows + 2 * halo_depth - 2 * margin
            center = solution_ext[:, :, 2 : 2 + extent]
            source_cut = source_ext[:, :, margin : margin + extent]
            potential_cut = potential_ext[:, :, margin : margin + extent]
            diagonal_cut = diagonal_ext[:, :, margin : margin + extent]
            inside_cut = inside[margin : margin + extent]
            solution_ext = (
                sweep(solution_ext, center, source_cut, potential_cut, diagonal_cut) * inside_cut
            )
        results.append(
            lax.psum(
                jnp.sum(weights[:, None, None, None] * orbitals[:, None] * solution_ext, axis=0),
                "orb",
            )
        )
    totals = jnp.stack(results, 0)
    owned = (owner == position).astype(jnp.float32)
    return (owned[:, None, None, None] * totals)[None]


def solution(mesh):
    in_specs = (
        P("orb", None, None, "grid", None),
        P("orb", "grid", None),
        P("grid", None),
        P("orb"),
        P("orb"),
        P(),
    )
    out_specs = P("orb", None, None, "grid", None)
    return jax.shard_map(shards, mesh=mesh, in_specs=in_specs, out_specs=out_specs, check_vma=False)
```

profile of v0, /device:TPU:0, one launch (start us, length us, event | category | flops | bytes accessed | tf_op | source)
XLA Modules:
  0.0 220.6 jit_solution(12964091721920774921)
XLA Ops:
  6.5 1.4 fusion.225
  9.2 1.9 select_bitcast_fusion.1
  11.4 75.5 %all-reduce.23.cloned.1.call-done = (f32[4,16,1024]{2,1,0:T(8,128)}, f32[4,16,1024]{2,1,0:T(8,128)}) async-done(((f32[4,16,1024]{2,1,0:T(8,128)}, f32[4,16,1024]{2,1,0:T(8,128)}), (f32[4,16,1024]{2,1,0:T(8,128)}, f32[4,16,1024]{2,1,0:T(8,128)})) %all-reduce.23.cloned.1.call-update) | async-done | bytes 524304 | tf_op jit(solution)/shard_map/psum | solution.py:33
  87.0 1.2 pad_maximum_fusion.5
  88.2 1.4 collective-permute-start
  89.6 1.3 collective-permute-start.1
  91.0 4.7 %collective-permute-start.2 = (f32[9,8,1024]{2,1,0:T(8,128)S(1)}, f32[9,8,1024]{2,1,0:T(8,128)S(1)}, u32[]{:S(2)}, u32[]{:S(2)}) collective-permute-start(f32[9,8,1024]{2,1,0:T(8,128)S(1)} %get-tuple-element.19), channel_id=1, source_target_pairs={{0,1},{1,2},{2,3},{4,5},{5,6},{6,7},{8,9},{9,10},{10,11},{12,13},{... | collective-permute-start | bytes 884744 | tf_op jit(solution)/shard_map/ppermute | solution.py:22
  95.7 1.3 collective-permute-start.3
  97.2 3.3 %collective-permute-done.3 = f32[9,8,1024]{2,1,0:T(8,128)S(1)} collective-permute-done((f32[9,8,1024]{2,1,0:T(8,128)S(1)}, f32[9,8,1024]{2,1,0:T(8,128)S(1)}, u32[]{:S(2)}, u32[]{:S(2)}) %collective-permute-start.3) | collective-permute-done | bytes 294944 | tf_op jit(solution)/shard_map/ppermute | solution.py:24
  100.4 0.2 fusion.157
  100.9 0.5 copy-done.4
  101.4 0.2 add_add_fusion.1
  101.5 0.3 broadcast_add_fusion.3
  102.6 0.6 multiply_negate_fusion.1
  103.2 0.4 slice.599
  103.6 4.8 %fusion.51 = f32[4,4,28,1024]{3,2,1,0:T(8,128)S(1)} fusion(f32[4,4,28,1024]{3,2,1,0:T(8,128)S(1)} %slice.599, f32[4,4,32,1024]{3,2,1,0:T(8,128)S(1)} %get-tuple-element.14, f32[4,4,32,1024]{3,2,1,0:T(8,128)S(1)} %get-tuple-element.13, f32[28]{0:T(128)S(1)} %slice.471, f32[4,28,1024]{2,1,0:T(8,128)S(1)} %slice_bitcast_fusion.2, ...), kind=kLoop, calls=%fused_computation.73 | loop fusion | flops 13762560 | bytes 13779056 | tf_op jit(solution)/shard_map/mul | solution.py:108
  108.4 0.2 slice.607
  108.6 3.5 %fusion.155 = f32[4,4,24,1024]{3,2,1,0:T(8,128)S(1)} fusion(f32[4,4,24,1024]{3,2,1,0:T(8,128)S(1)} %slice.607, f32[4,4,28,1024]{3,2,1,0:T(8,128)S(1)} %fusion.51, f32[4,4,32,1024]{3,2,1,0:T(8,128)S(1)} %get-tuple-element.13, f32[24]{0:T(128)S(1)} %slice.488, f32[4,24,1024]{2,1,0:T(8,128)S(1)} %slice_bitcast_fusion.10, ...), kind=kLoop, calls=%fused_computation.219 | loop fusion | flops 11796480 | bytes 11812960 | tf_op jit(solution)/shard_map/mul | solution.py:108
  112.2 0.2 slice.615
  112.4 3.5 %fusion.154 = f32[4,4,20,1024]{3,2,1,0:T(8,128)S(1)} fusion(f32[4,4,20,1024]{3,2,1,0:T(8,128)S(1)} %slice.615, f32[4,4,24,1024]{3,2,1,0:T(8,128)S(1)} %fusion.155, f32[4,4,32,1024]{3,2,1,0:T(8,128)S(1)} %get-tuple-element.13, f32[20]{0:T(128)S(1)} %slice.505, f32[4,20,1024]{2,1,0:T(8,128)S(1)} %slice_bitcast_fusion.8, ...), kind=kLoop, calls=%fused_computation.218 | loop fusion | flops 9830400 | bytes 9846864 | tf_op jit(solution)/shard_map/mul | solution.py:108
  115.9 0.2 slice.623
  116.1 0.6 multiply_negate_fusion
  116.6 0.4 slice.636
  117.1 4.6 %fusion.50 = f32[4,4,28,1024]{3,2,1,0:T(8,128)S(1)} fusion(f32[4,4,28,1024]{3,2,1,0:T(8,128)S(1)} %slice.636, f32[4,4,32,1024]{3,2,1,0:T(8,128)S(1)} %get-tuple-element.16, f32[4,4,32,1024]{3,2,1,0:T(8,128)S(1)} %get-tuple-element.15, f32[4,28,1024]{2,1,0:T(8,128)S(1)} %slice_bitcast_fusion, f32[4,28,1024]{2,1,0:T(8,128)S(1)} %slice_bitcast_fusion.1, ...), kind=kLoop, calls=%fused_computation.72 | loop fusion | flops 13762560 | bytes 13779056 | tf_op jit(solution)/shard_map/mul | solution.py:108
  121.7 0.2 slice.644
  121.9 3.5 %fusion.153 = f32[4,4,24,1024]{3,2,1,0:T(8,128)S(1)} fusion(f32[4,4,24,1024]{3,2,1,0:T(8,128)S(1)} %slice.644, f32[4,4,28,1024]{3,2,1,0:T(8,128)S(1)} %fusion.50, f32[4,4,32,1024]{3,2,1,0:T(8,128)S(1)} %get-tuple-element.15, f32[4,24,1024]{2,1,0:T(8,128)S(1)} %slice_bitcast_fusion.6, f32[4,24,1024]{2,1,0:T(8,128)S(1)} %slice_bitcast_fusion.7, ...), kind=kLoop, calls=%fused_computation.217 | loop fusion | flops 11796480 | bytes 11812960 | tf_op jit(solution)/shard_map/mul | solution.py:108
  125.4 0.3 slice.652
  125.7 3.7 %fusion.152 = f32[4,4,20,1024]{3,2,1,0:T(8,128)S(1)} fusion(f32[4,4,20,1024]{3,2,1,0:T(8,128)S(1)} %slice.652, f32[4,4,24,1024]{3,2,1,0:T(8,128)S(1)} %fusion.153, f32[4,4,32,1024]{3,2,1,0:T(8,128)S(1)} %get-tuple-element.15, f32[4,20,1024]{2,1,0:T(8,128)S(1)} %slice_bitcast_fusion.4, f32[4,20,1024]{2,1,0:T(8,128)S(1)} %slice_bitcast_fusion.5, ...), kind=kLoop, calls=%fused_computation.216 | loop fusion | flops 9830400 | bytes 9846864 | tf_op jit(solution)/shard_map/mul | solution.py:108
  129.5 3.1 %multiply_reduce_fusion.1 = f32[4,16,1024]{2,1,0:T(8,128)} fusion(f32[4,4,16,1024]{3,2,1,0:T(8,128)S(1)} %slice.623, f32[4,4,20,1024]{3,2,1,0:T(8,128)S(1)} %fusion.154, f32[4,4,32,1024]{3,2,1,0:T(8,128)S(1)} %get-tuple-element.13, f32[16]{0:T(128)S(1)} %slice.522, f32[4,16,1024]{2,1,0:T(8,128)S(1)} %slice_bitcast_fusion.14, ...), kind=kLoop, calls=%fused_computation.298 | loop fusion | flops 8323072 | bytes 7356480 | tf_op jit(solution)/shard_map/reduce_sum | solution.py:112
  132.7 3.1 %multiply_reduce_fusion = f32[4,16,1024]{2,1,0:T(8,128)} fusion(f32[4,4,16,1024]{3,2,1,0:T(8,128)S(1)} %slice.660, f32[4,4,20,1024]{3,2,1,0:T(8,128)S(1)} %fusion.152, f32[4,4,32,1024]{3,2,1,0:T(8,128)S(1)} %get-tuple-element.15, f32[4,16,1024]{2,1,0:T(8,128)S(1)} %slice_bitcast_fusion.12, f32[4,16,1024]{2,1,0:T(8,128)S(1)} %slice_bitcast_fusion.13, ...), kind=kLoop, calls=%fused_computation.296 | loop fusion | flops 8323072 | bytes 7356480 | tf_op jit(solution)/shard_map/reduce_sum | solution.py:112
  135.8 76.0 %all-reduce.21.cloned.1.call-done = (f32[1,1,4,16,1024]{4,3,2,1,0:T(8,128)}, f32[1,1,4,16,1024]{4,3,2,1,0:T(8,128)}) async-done(((f32[1,1,4,16,1024]{4,3,2,1,0:T(8,128)}, f32[1,1,4,16,1024]{4,3,2,1,0:T(8,128)}), (f32[1,1,4,16,1024]{4,3,2,1,0:T(8,128)}, f32[1,1,4,16,1024]{4,3,2,1,0:T(8,128)})) %all-reduce.21.cloned.1.call-update) | async-done | bytes 524304 | tf_op jit(solution)/shard_map/psum | solution.py:111
  211.8 1.9 maximum_multiply_fusion
  (51 shorter events, 1.5 us)
Async XLA Ops:
  6.5 4.9 %copy-start.6 = (s32[4]{0:T(128)S(1)}, s32[4]{0:T(128)}, u32[]{:S(2)}) copy-start(s32[4]{0:T(128)} %param.10) | copy-start | bytes 52
  6.5 80.4 %copy-start.3 = (f32[16,1024]{1,0:T(8,128)S(1)}, f32[16,1024]{1,0:T(8,128)}, u32[]{:S(2)}) copy-start(f32[16,1024]{1,0:T(8,128)} %param.8) | copy-start | bytes 196612
  6.5 80.4 %copy-start = (f32[4,16,1024]{2,1,0:T(8,128)S(1)}, f32[4,16,1024]{2,1,0:T(8,128)}, u32[]{:S(2)}) copy-start(f32[4,16,1024]{2,1,0:T(8,128)} %param.7) | copy-start | bytes 786436
  6.5 80.4 %all-reduce.23.cloned.1.call-start = ((), (), s32[]{:S(2)}) async-start(), calls=%async_computation.1 | async-start | bytes 1048576 | tf_op jit(solution)/shard_map/psum | solution.py:33
  11.1 200.8 %all-reduce.21.cloned.1.call-start = ((), (), s32[]{:S(2)}) async-start(), calls=%async_computation | async-start | bytes 1048576 | tf_op jit(solution)/shard_map/psum | solution.py:111
  88.1 12.3 %copy-start.1 = (f32[4,16,1024]{2,1,0:T(8,128)S(1)}, f32[4,16,1024]{2,1,0:T(8,128)}, u32[]{:S(2)}) copy-start(f32[4,16,1024]{2,1,0:T(8,128)} %get-tuple-element.7) | copy-start | bytes 786436
  88.1 12.3 %copy-start.2 = (f32[4,16,1024]{2,1,0:T(8,128)S(1)}, f32[4,16,1024]{2,1,0:T(8,128)}, u32[]{:S(2)}) copy-start(f32[4,16,1024]{2,1,0:T(8,128)} %get-tuple-element.8) | copy-start | bytes 786436
  88.2 9.0 %collective-permute-start = (f32[9,8,1024]{2,1,0:T(8,128)S(1)}, f32[9,8,1024]{2,1,0:T(8,128)S(1)}, u32[]{:S(2)}, u32[]{:S(2)}) collective-permute-start(f32[9,8,1024]{2,1,0:T(8,128)S(1)} %get-tuple-element.17), channel_id=1, source_target_pairs={{0,1},{1,2},{2,3},{4,5},{5,6},{6,7},{8,9},{9,10},{10,11},{12,13},{... | collective-permute-start | bytes 884744 | tf_op jit(solution)/shard_map/ppermute | solution.py:22
  89.6 7.5 %collective-permute-start.1 = (f32[9,8,1024]{2,1,0:T(8,128)S(1)}, f32[9,8,1024]{2,1,0:T(8,128)S(1)}, u32[]{:S(2)}, u32[]{:S(2)}) collective-permute-start(f32[9,8,1024]{2,1,0:T(8,128)S(1)} %get-tuple-element.18), channel_id=1, source_target_pairs={{1,0},{2,1},{3,2},{5,4},{6,5},{7,6},{9,8},{10,9},{11,10},{13,12},{... | collective-permute-start | bytes 884744 | tf_op jit(solution)/shard_map/ppermute | solution.py:24
  91.0 6.2 %collective-permute-start.2 = (f32[9,8,1024]{2,1,0:T(8,128)S(1)}, f32[9,8,1024]{2,1,0:T(8,128)S(1)}, u32[]{:S(2)}, u32[]{:S(2)}) collective-permute-start(f32[9,8,1024]{2,1,0:T(8,128)S(1)} %get-tuple-element.19), channel_id=1, source_target_pairs={{0,1},{1,2},{2,3},{4,5},{5,6},{6,7},{8,9},{9,10},{10,11},{12,13},{... | collective-permute-start | bytes 884744 | tf_op jit(solution)/shard_map/ppermute | solution.py:22
  95.7 4.7 %collective-permute-start.3 = (f32[9,8,1024]{2,1,0:T(8,128)S(1)}, f32[9,8,1024]{2,1,0:T(8,128)S(1)}, u32[]{:S(2)}, u32[]{:S(2)}) collective-permute-start(f32[9,8,1024]{2,1,0:T(8,128)S(1)} %get-tuple-element.20), channel_id=1, source_target_pairs={{1,0},{2,1},{3,2},{5,4},{6,5},{7,6},{9,8},{10,9},{11,10},{13,12},{... | collective-permute-start | bytes 884744 | tf_op jit(solution)/shard_map/ppermute | solution.py:24
  100.7 0.7 copy-start.4
  132.7 3.1 %copy-start.5 = (s32[2]{0:T(128)S(1)}, s32[2]{0:T(128)}, u32[]{:S(2)}) copy-start(s32[2]{0:T(128)} %param.11) | copy-start | bytes 28
Sparse Core Ops, SparseCore 0:
  11.2 75.7 all-reduce.22
  135.9 75.8 all-reduce.20
where the time goes:
time: 221 us
  waiting for transfers between devices  155 us (70%)
  other arithmetic  36.9 us (17%)
  between operations  15.1 us (7%)
  starting transfers between devices  8.81 us (4%)
  local copies, waits for them, and re-layouts  5.03 us (2%)
    psum x1, waiting for transfers between devices, shards(): lax.psum(jnp.sum(weights[:, None, None, None] * orbitals[:, None] * solut...  76 us
    psum x1, waiting for transfers between devices, from_root(): return lax.psum(kept, axis)  75.5 us
    mul x6, other arithmetic, shards(): sweep(solution_ext, center, source_cut, potential_cut, diagonal_cut)  23.7 us
    reduce_sum x2, other arithmetic, shards(): jnp.sum(weights[:, None, None, None] * orbitals[:, None] * solution_ext,...  6.25 us
    ppermute x2, starting transfers between devices, with_halo(): lax.ppermute(tail, axis, [(i, (i + 1) % count) for i in range(ends)])  6.18 us
  transfers between devices with their start and end apart: 6, of which 3 were waited for; matrix products, arithmetic and copies ran while one was open for 0% of the time, Pallas kernels for 0%

commit v1 on v0

--- a/solution.py
+++ b/solution.py
@@ -30,7 +30,7 @@
 
 def from_root(value, axis, source):
     kept = jnp.where(lax.axis_index(axis) == source, value, 0).astype(value.dtype)
-    return lax.psum(kept, axis)
+    return jnp.sum(lax.all_gather(kept, axis), axis=0)
 
 
 def laplacian(padded, solution):

time: 221 us -> 246 us (1.11)
  waiting for transfers between devices: 155 us -> 178 us
    all_gather x0 -> x2, waiting for transfers between devices: none -> 98.8 us  [from_root(): return jnp.sum(lax.all_gather(kept, axis), axis=0)]
    psum x1 -> x0, waiting for transfers between devices: 75.5 us -> none  [from_root(): return lax.psum(kept, axis)]
    reduce_sum x0 -> x2, other arithmetic: none -> 3.49 us  [from_root(): return jnp.sum(lax.all_gather(kept, axis), axis=0)]
  transfers between devices with their start and end apart: 6 -> 7, of which waited for: 3 -> 4; matrix products, arithmetic and copies ran while one was open for 0% -> 1% of each run, Pallas kernels for 0% -> 0%
where the time goes in v1:
time: 246 us
  waiting for transfers between devices  178 us (72%)
  other arithmetic  39.3 us (16%)
  between operations  14.9 us (6%)
  starting transfers between devices  8.71 us (4%)
  local copies, waits for them, and re-layouts  5.08 us (2%)
    all_gather x2, waiting for transfers between devices, from_root(): return jnp.sum(lax.all_gather(kept, axis), axis=0)  98.8 us
    psum x1, waiting for transfers between devices, shards(): lax.psum(jnp.sum(weights[:, None, None, None] * orbitals[:, None] * solut...  75.3 us
    mul x6, other arithmetic, shards(): sweep(solution_ext, center, source_cut, potential_cut, diagonal_cut)  23.6 us
    reduce_sum x2, other arithmetic, shards(): jnp.sum(weights[:, None, None, None] * orbitals[:, None] * solution_ext,...  6.24 us
    ppermute x2, starting transfers between devices, with_halo(): lax.ppermute(tail, axis, [(i, (i + 1) % count) for i in range(ends)])  6.04 us
  transfers between devices with their start and end apart: 7, of which 4 were waited for; matrix products, arithmetic and copies ran while one was open for 1% of the time, Pallas kernels for 0%

profile of v1, /device:TPU:0, one launch (start us, length us, event | category | flops | bytes accessed | tf_op | source)
XLA Modules:
  0.0 246.2 jit_solution(9486669123672844221)
XLA Ops:
  6.5 1.4 fusion.225
  9.3 1.9 slice_select_fusion.1
  11.2 0.7 all-gather.7.cloned.1.call-update
  12.3 50.8 %all-gather.5.cloned.1.call-done = f32[8,1,4,16,1024]{4,3,2,1,0:T(8,128)} async-done(((f32[1,1,4,16,1024]{4,3,2,1,0:T(8,128)}), f32[8,1,4,16,1024]{4,3,2,1,0:T(8,128)}) %all-gather.5.cloned.1.call-update) | async-done | bytes 2097168 | tf_op jit(solution)/shard_map/all_gather | solution.py:33
  63.1 1.7 reduce_sum.36
  64.9 48.0 %all-gather.7.cloned.1.call-done = f32[8,1,4,16,1024]{4,3,2,1,0:T(8,128)} async-done(((f32[1,1,4,16,1024]{4,3,2,1,0:T(8,128)}), f32[8,1,4,16,1024]{4,3,2,1,0:T(8,128)}) %all-gather.7.cloned.1.call-update) | async-done | bytes 2097168 | tf_op jit(solution)/shard_map/all_gather | solution.py:33
  112.9 1.7 reduce_sum.38
  114.9 1.3 collective-permute-start
  116.2 1.3 collective-permute-start.1
  117.5 4.7 %collective-permute-start.2 = (f32[9,8,1024]{2,1,0:T(8,128)S(1)}, f32[9,8,1024]{2,1,0:T(8,128)S(1)}, u32[]{:S(2)}, u32[]{:S(2)}) collective-permute-start(f32[9,8,1024]{2,1,0:T(8,128)S(1)} %get-tuple-element.17), channel_id=1, source_target_pairs={{0,1},{1,2},{2,3},{4,5},{5,6},{6,7},{8,9},{9,10},{10,11},{12,13},{... | collective-permute-start | bytes 884744 | tf_op jit(solution)/shard_map/ppermute | solution.py:22
  122.3 1.3 collective-permute-start.3
  123.7 3.3 %collective-permute-done.3 = f32[9,8,1024]{2,1,0:T(8,128)S(1)} collective-permute-done((f32[9,8,1024]{2,1,0:T(8,128)S(1)}, f32[9,8,1024]{2,1,0:T(8,128)S(1)}, u32[]{:S(2)}, u32[]{:S(2)}) %collective-permute-start.3) | collective-permute-done | bytes 294944 | tf_op jit(solution)/shard_map/ppermute | solution.py:24
  127.0 0.3 fusion.157
  127.3 0.2 fusion.221
  127.5 0.4 copy-done.2
  128.1 0.3 broadcast_add_fusion.3
  129.2 0.6 multiply_negate_fusion.1
  129.8 0.4 slice.599
  130.2 4.8 %fusion.51 = f32[4,4,28,1024]{3,2,1,0:T(8,128)S(1)} fusion(f32[4,4,28,1024]{3,2,1,0:T(8,128)S(1)} %slice.599, f32[4,4,32,1024]{3,2,1,0:T(8,128)S(1)} %get-tuple-element.12, f32[4,4,32,1024]{3,2,1,0:T(8,128)S(1)} %get-tuple-element.11, f32[28]{0:T(128)S(1)} %slice.471, f32[4,28,1024]{2,1,0:T(8,128)S(1)} %slice_bitcast_fusion.2, ...), kind=kLoop, calls=%fused_computation.73 | loop fusion | flops 13762560 | bytes 13779056 | tf_op jit(solution)/shard_map/mul | solution.py:108
  135.0 0.3 slice.607
  135.3 3.5 %fusion.155 = f32[4,4,24,1024]{3,2,1,0:T(8,128)S(1)} fusion(f32[4,4,24,1024]{3,2,1,0:T(8,128)S(1)} %slice.607, f32[4,4,28,1024]{3,2,1,0:T(8,128)S(1)} %fusion.51, f32[4,4,32,1024]{3,2,1,0:T(8,128)S(1)} %get-tuple-element.11, f32[24]{0:T(128)S(1)} %slice.488, f32[4,24,1024]{2,1,0:T(8,128)S(1)} %slice_bitcast_fusion.10, ...), kind=kLoop, calls=%fused_computation.219 | loop fusion | flops 11796480 | bytes 11812960 | tf_op jit(solution)/shard_map/mul | solution.py:108
  138.8 0.2 slice.615
  139.0 3.5 %fusion.154 = f32[4,4,20,1024]{3,2,1,0:T(8,128)S(1)} fusion(f32[4,4,20,1024]{3,2,1,0:T(8,128)S(1)} %slice.615, f32[4,4,24,1024]{3,2,1,0:T(8,128)S(1)} %fusion.155, f32[4,4,32,1024]{3,2,1,0:T(8,128)S(1)} %get-tuple-element.11, f32[20]{0:T(128)S(1)} %slice.505, f32[4,20,1024]{2,1,0:T(8,128)S(1)} %slice_bitcast_fusion.8, ...), kind=kLoop, calls=%fused_computation.218 | loop fusion | flops 9830400 | bytes 9846864 | tf_op jit(solution)/shard_map/mul | solution.py:108
  142.7 0.6 multiply_negate_fusion
  143.3 0.4 slice.636
  143.7 4.6 %fusion.50 = f32[4,4,28,1024]{3,2,1,0:T(8,128)S(1)} fusion(f32[4,4,28,1024]{3,2,1,0:T(8,128)S(1)} %slice.636, f32[4,4,32,1024]{3,2,1,0:T(8,128)S(1)} %get-tuple-element.14, f32[4,4,32,1024]{3,2,1,0:T(8,128)S(1)} %get-tuple-element.13, f32[4,28,1024]{2,1,0:T(8,128)S(1)} %slice_bitcast_fusion, f32[4,28,1024]{2,1,0:T(8,128)S(1)} %slice_bitcast_fusion.1, ...), kind=kLoop, calls=%fused_computation.72 | loop fusion | flops 13762560 | bytes 13779056 | tf_op jit(solution)/shard_map/mul | solution.py:108
  148.5 3.5 %fusion.153 = f32[4,4,24,1024]{3,2,1,0:T(8,128)S(1)} fusion(f32[4,4,24,1024]{3,2,1,0:T(8,128)S(1)} %slice.644, f32[4,4,28,1024]{3,2,1,0:T(8,128)S(1)} %fusion.50, f32[4,4,32,1024]{3,2,1,0:T(8,128)S(1)} %get-tuple-element.13, f32[4,24,1024]{2,1,0:T(8,128)S(1)} %slice_bitcast_fusion.6, f32[4,24,1024]{2,1,0:T(8,128)S(1)} %slice_bitcast_fusion.7, ...), kind=kLoop, calls=%fused_computation.217 | loop fusion | flops 11796480 | bytes 11812960 | tf_op jit(solution)/shard_map/mul | solution.py:108
  152.3 3.7 %fusion.152 = f32[4,4,20,1024]{3,2,1,0:T(8,128)S(1)} fusion(f32[4,4,20,1024]{3,2,1,0:T(8,128)S(1)} %slice.652, f32[4,4,24,1024]{3,2,1,0:T(8,128)S(1)} %fusion.153, f32[4,4,32,1024]{3,2,1,0:T(8,128)S(1)} %get-tuple-element.13, f32[4,20,1024]{2,1,0:T(8,128)S(1)} %slice_bitcast_fusion.4, f32[4,20,1024]{2,1,0:T(8,128)S(1)} %slice_bitcast_fusion.5, ...), kind=kLoop, calls=%fused_computation.216 | loop fusion | flops 9830400 | bytes 9846864 | tf_op jit(solution)/shard_map/mul | solution.py:108
  156.1 3.1 %multiply_reduce_fusion.1 = f32[4,16,1024]{2,1,0:T(8,128)} fusion(f32[4,4,16,1024]{3,2,1,0:T(8,128)S(1)} %slice.623, f32[4,4,20,1024]{3,2,1,0:T(8,128)S(1)} %fusion.154, f32[4,4,32,1024]{3,2,1,0:T(8,128)S(1)} %get-tuple-element.11, f32[16]{0:T(128)S(1)} %slice.522, f32[4,16,1024]{2,1,0:T(8,128)S(1)} %slice_bitcast_fusion.14, ...), kind=kLoop, calls=%fused_computation.298 | loop fusion | flops 8323072 | bytes 7356480 | tf_op jit(solution)/shard_map/reduce_sum | solution.py:112
  159.3 3.1 %multiply_reduce_fusion = f32[4,16,1024]{2,1,0:T(8,128)} fusion(f32[4,4,16,1024]{3,2,1,0:T(8,128)S(1)} %slice.660, f32[4,4,20,1024]{3,2,1,0:T(8,128)S(1)} %fusion.152, f32[4,4,32,1024]{3,2,1,0:T(8,128)S(1)} %get-tuple-element.13, f32[4,16,1024]{2,1,0:T(8,128)S(1)} %slice_bitcast_fusion.12, f32[4,16,1024]{2,1,0:T(8,128)S(1)} %slice_bitcast_fusion.13, ...), kind=kLoop, calls=%fused_computation.296 | loop fusion | flops 8323072 | bytes 7356480 | tf_op jit(solution)/shard_map/reduce_sum | solution.py:112
  162.4 75.3 %all-reduce.19.cloned.1.call-done = (f32[1,1,4,16,1024]{4,3,2,1,0:T(8,128)}, f32[1,1,4,16,1024]{4,3,2,1,0:T(8,128)}) async-done(((f32[1,1,4,16,1024]{4,3,2,1,0:T(8,128)}, f32[1,1,4,16,1024]{4,3,2,1,0:T(8,128)}), (f32[1,1,4,16,1024]{4,3,2,1,0:T(8,128)}, f32[1,1,4,16,1024]{4,3,2,1,0:T(8,128)})) %all-reduce.19.cloned.1.call-update) | async-done | bytes 524304 | tf_op jit(solution)/shard_map/psum | solution.py:111
  237.7 1.9 maximum_multiply_fusion
  (52 shorter events, 2.3 us)
Async XLA Ops:
  6.5 5.8 %copy-start.4 = (s32[4]{0:T(128)S(1)}, s32[4]{0:T(128)}, u32[]{:S(2)}) copy-start(s32[4]{0:T(128)} %param.10) | copy-start | bytes 52
  6.5 56.6 %all-gather.5.cloned.1.call-start = ((), (), s32[]{:S(2)}) async-start(), calls=%async_computation | async-start | bytes 2359296 | tf_op jit(solution)/shard_map/all_gather | solution.py:33
  11.2 101.7 %all-gather.7.cloned.1.call-start = ((), (), s32[]{:S(2)}) async-start(), calls=%async_computation.1 | async-start | bytes 2359296 | tf_op jit(solution)/shard_map/all_gather | solution.py:33
  11.9 225.8 %all-reduce.19.cloned.1.call-start = ((), (), s32[]{:S(2)}) async-start(), calls=%async_computation.2 | async-start | bytes 1048576 | tf_op jit(solution)/shard_map/psum | solution.py:111
  64.9 49.8 %copy-start = (f32[4,16,1024]{2,1,0:T(8,128)S(1)}, f32[4,16,1024]{2,1,0:T(8,128)}, u32[]{:S(2)}) copy-start(f32[4,16,1024]{2,1,0:T(8,128)} %param.7) | copy-start | bytes 786436
  64.9 49.8 %copy-start.1 = (f32[16,1024]{1,0:T(8,128)S(1)}, f32[16,1024]{1,0:T(8,128)}, u32[]{:S(2)}) copy-start(f32[16,1024]{1,0:T(8,128)} %param.8) | copy-start | bytes 196612
  114.9 8.8 %collective-permute-start = (f32[9,8,1024]{2,1,0:T(8,128)S(1)}, f32[9,8,1024]{2,1,0:T(8,128)S(1)}, u32[]{:S(2)}, u32[]{:S(2)}) collective-permute-start(f32[9,8,1024]{2,1,0:T(8,128)S(1)} %get-tuple-element.15), channel_id=1, source_target_pairs={{0,1},{1,2},{2,3},{4,5},{5,6},{6,7},{8,9},{9,10},{10,11},{12,13},{... | collective-permute-start | bytes 884744 | tf_op jit(solution)/shard_map/ppermute | solution.py:22
  116.2 7.5 %collective-permute-start.1 = (f32[9,8,1024]{2,1,0:T(8,128)S(1)}, f32[9,8,1024]{2,1,0:T(8,128)S(1)}, u32[]{:S(2)}, u32[]{:S(2)}) collective-permute-start(f32[9,8,1024]{2,1,0:T(8,128)S(1)} %get-tuple-element.16), channel_id=1, source_target_pairs={{1,0},{2,1},{3,2},{5,4},{6,5},{7,6},{9,8},{10,9},{11,10},{13,12},{... | collective-permute-start | bytes 884744 | tf_op jit(solution)/shard_map/ppermute | solution.py:24
  117.5 6.2 %collective-permute-start.2 = (f32[9,8,1024]{2,1,0:T(8,128)S(1)}, f32[9,8,1024]{2,1,0:T(8,128)S(1)}, u32[]{:S(2)}, u32[]{:S(2)}) collective-permute-start(f32[9,8,1024]{2,1,0:T(8,128)S(1)} %get-tuple-element.17), channel_id=1, source_target_pairs={{0,1},{1,2},{2,3},{4,5},{5,6},{6,7},{8,9},{9,10},{10,11},{12,13},{... | collective-permute-start | bytes 884744 | tf_op jit(solution)/shard_map/ppermute | solution.py:22
  122.3 4.7 %collective-permute-start.3 = (f32[9,8,1024]{2,1,0:T(8,128)S(1)}, f32[9,8,1024]{2,1,0:T(8,128)S(1)}, u32[]{:S(2)}, u32[]{:S(2)}) collective-permute-start(f32[9,8,1024]{2,1,0:T(8,128)S(1)} %get-tuple-element.18), channel_id=1, source_target_pairs={{1,0},{2,1},{3,2},{5,4},{6,5},{7,6},{9,8},{10,9},{11,10},{13,12},{... | collective-permute-start | bytes 884744 | tf_op jit(solution)/shard_map/ppermute | solution.py:24
  127.3 0.7 copy-start.2
  159.3 3.1 %copy-start.3 = (s32[2]{0:T(128)S(1)}, s32[2]{0:T(128)}, u32[]{:S(2)}) copy-start(s32[2]{0:T(128)} %param.11) | copy-start | bytes 28
Sparse Core Ops, SparseCore 0:
  11.3 51.7 all-gather.4
  65.3 47.6 all-gather.6
  162.5 75.1 all-reduce.18
